TPU v7x, 32 devices: a whole 2x2x4 slice. The times are simulated.
32 devices in a mesh: fibre: 2 (over y), chan: 4 (over z), win: 2 (over x), freq: 2 (over core).
Axes of the slice: x: 2, y: 2, z: 4, core: 2. Of those that a mesh axis runs over, the one named last changes fastest.
Arguments:
- spectra: bfloat16 [16, 2, 64, 2048], P('win', None, ('fibre', 'chan'), 'freq'), parts along dimension 2, may hold values from -50 to 50
- keep: int32 [32], P(('fibre', 'win')), parts along dimension 0, may hold values 0 or 1
- pair_mask: int32 [64, 4], P(('fibre', 'chan')), parts along dimension 0, may hold values 0 or 1
Outputs:
- correlations: float32 [64, 4, 8, 1024], P(('fibre', 'chan'), None, None, ('win', 'freq')), parts along dimension 0
There are 2 independent parts, one for each index of `fibre`. A program takes and returns all parts, laid end to end along the dimension named above; each array names one. Nothing has to cross between parts.
All inputs are finite; a program needn't handle non-finite values. No bound on the sum of `keep` or of `pair_mask` on one device may be relied on, other than what follows from the above.
Results may differ from a plain program's by a relative error of at most 0.0014.
Values may be sent and summed in bfloat16 or wider, within the bound.
A program may use at most 128 MiB of HBM per device.

v0:
```python
import math

import jax
import jax.numpy as jnp
from jax import lax
from jax.sharding import PartitionSpec as P

LAGS = 1024
F_LO = 60
NSAMP = 15000


EPS = 1e-06


def from_behind(block, axis, distance):
    devices = range(lax.axis_size(axis))
    route = [(i - distance, i) for i in devices if i - distance in devices]
    return lax.ppermute(block, axis, route)


def lag_table(start, count):
    bins = F_LO + start + jnp.arange(count, dtype=jnp.int32)
    offsets = jnp.arange(LAGS, dtype=jnp.int32) - LAGS // 2
    turns = jnp.remainder(bins[:, None] * offsets[None, :], NSAMP).astype(jnp.float32)
    angle = turns * (2.0 * math.pi / NSAMP)
    return jnp.concatenate([jnp.cos(angle), -jnp.sin(angle)], axis=0)


def local(spectra, keep, pair_mask):
    w_dev, _, ch_dev, f_dev = spectra.shape
    reach = pair_mask.shape[1] - 1
    n_freq = lax.axis_size("freq")
    n_win = lax.axis_size("win")
    spec = spectra.astype(jnp.float32)
    partial_power = jnp.sum(spec * spec, axis=(1, 3))
    power = lax.psum(partial_power, "freq") / (f_dev * n_freq)
    white = (spec * lax.rsqrt(power + EPS)[:, None, :, None]).astype(jnp.bfloat16)
    own = white * keep.astype(jnp.bfloat16)[:, None, None, None]
    swapped = jnp.concatenate([own[:, 1:2], -own[:, 0:1]], axis=1)
    partners = [white]
    moving = white
    for step in range(reach):
        moving = from_behind(moving, "chan", -1)
        partners.append(moving)
    stacked = jnp.stack(partners, axis=2)
    real_part = jnp.einsum("wcif,wckjf->ikjf", own, stacked, preferred_element_type=jnp.float32)
    imag_part = jnp.einsum("wcif,wckjf->ikjf", swapped, stacked, preferred_element_type=jnp.float32)
    cross = jnp.stack([real_part, imag_part], axis=3)
    table = lag_table(lax.axis_index("freq") * f_dev, f_dev)
    partial_value = jnp.dot(cross.reshape(-1, 2 * f_dev), table, precision=lax.Precision.HIGHEST)
    partial_value = partial_value.reshape(ch_dev, reach + 1, ch_dev, LAGS)
    lagsum = lax.psum_scatter(partial_value, ("win", "freq"), scatter_dimension=3, tiled=True)
    scale = 1.0 / math.sqrt(w_dev * n_win * f_dev * n_freq)
    return lagsum * scale * pair_mask.astype(jnp.float32)[:, :, None, None]


def solution(mesh):
    in_specs = (
        P("win", None, ("fibre", "chan"), "freq"),
        P(("fibre", "win")),
        P(("fibre", "chan"), None),
    )
    out_specs = P(("fibre", "chan"), None, None, ("win", "freq"))
    return jax.shard_map(local, mesh=mesh, in_specs=in_specs, out_specs=out_specs, check_vma=False)
```

profile of v0, /device:TPU:1, one launch (start us, length us, event | category | flops | bytes accessed | tf_op | source)
XLA Modules:
  0.0 170.7 jit_solution(4858289674584898826)
XLA Ops:
  6.5 0.0 reduce-scatter.2.cloned.1.call-start
  6.5 1.1 fusion.9
  7.6 2.5 %psum.7 = f32[8,8]{1,0:T(8,128)S(1)} all-reduce(f32[8,8]{1,0:T(8,128)S(1)} %fusion.9), channel_id=1, replica_groups=mesh['fibre'=2,'chan'=4,'win'=2,'freq'=2] {'freq'}, use_global_device_ids=true, to_apply=%region_1.0 | all-reduce | flops 64 | bytes 512 | tf_op jit(solution)/shard_map/psum | solution.py:37
  10.1 0.7 convert_element_type.17
  10.8 1.1 broadcast_multiply_fusion.1
  11.9 1.3 collective-permute-start
  13.2 9.4 %collective-permute-done = bf16[8,2,8,1024]{3,2,1,0:T(8,128)(2,1)S(1)} collective-permute-done((bf16[8,2,8,1024]{3,2,1,0:T(8,128)(2,1)S(1)}, bf16[8,2,8,1024]{3,2,1,0:T(8,128)(2,1)S(1)}, u32[]{:S(2)}, u32[]{:S(2)}) %collective-permute-start) | collective-permute-done | bytes 262176 | tf_op jit(solution)/shard_map/ppermute | solution.py:19
  22.5 1.3 collective-permute-start.1
  23.9 4.7 %copy.59 = bf16[8,2,8,1024,1]{2,0,1,4,3:T(8,128)(2,1)} copy(bf16[8,2,8,1024,1]{3,2,1,0,4:T(8,128)(2,1)S(1)} %maximum_bitcast_fusion.2) | data formatting | bytes 524288 | tf_op jit(solution)/shard_map/concatenate | solution.py:40
  28.6 4.7 %copy.57 = bf16[8,2,8,1024,1]{2,0,1,4,3:T(8,128)(2,1)} copy(bf16[8,2,8,1024,1]{3,2,1,0,4:T(8,128)(2,1)S(1)} %bitcast.33) | data formatting | bytes 524288 | tf_op jit(solution)/shard_map/mul | solution.py:39
  33.3 0.0 collective-permute-done.1
  33.3 1.3 collective-permute-start.2
  34.5 19.5 %fusion.7 = (f32[1024,1024]{1,0:T(8,128)}, f32[1024,1024]{1,0:T(8,128)}) fusion(s32[1024]{0:T(1024)S(1)} %get-tuple-element.11, s32[1024]{0:T(1024)S(1)} %get-tuple-element.12), kind=kLoop, calls=%fused_computation.13 | loop fusion | flops 10485760 | bytes 8396800 | tf_op jit(solution)/shard_map/cos | solution.py:27
  54.0 0.0 collective-permute-done.2
  54.0 0.1 pad_maximum_fusion.1
  54.2 22.7 %copy.50 = bf16[8,2,4,8,1024]{0,3,1,2,4:T(8,128)(2,1)} copy(bf16[8,2,4,8,1024]{4,3,1,0,2:T(8,128)(2,1)S(1)} %pad_maximum_fusion.1) | data formatting | bytes 2097152 | tf_op jit(solution)/shard_map/stack | solution.py:46
  76.9 12.5 %convolution_bitcast_fusion = f32[8,4,8,1,1024]{0,2,1,4,3:T(8,128)} fusion(bf16[8,2,4,8,1024]{0,3,1,2,4:T(8,128)(2,1)} %copy.50, bf16[8,2,8,1024,1]{2,0,1,4,3:T(8,128)(2,1)} %copy.59), kind=kOutput, calls=%fused_computation | convolution fusion | flops 8388608 | bytes 2359296 | tf_op jit(solution)/shard_map/wcif,wckjf->ikjf/dot_general | solution.py:48
  89.3 9.9 %copy.55 = f32[8,4,8,1,1024]{4,2,3,1,0:T(8,128)S(1)} copy(f32[8,4,8,1,1024]{0,2,1,4,3:T(8,128)} %convolution_bitcast_fusion) | data formatting | bytes 2097152 | tf_op jit(solution)/shard_map/stack | solution.py:49
  99.2 12.4 %convolution_bitcast_fusion.1 = f32[8,4,8,1,1024]{0,2,1,4,3:T(8,128)} fusion(bf16[8,2,4,8,1024]{0,3,1,2,4:T(8,128)(2,1)} %copy.50, bf16[8,2,8,1024,1]{2,0,1,4,3:T(8,128)(2,1)} %copy.57), kind=kOutput, calls=%fused_computation.1 | convolution fusion | flops 8388608 | bytes 2359296 | tf_op jit(solution)/shard_map/wcif,wckjf->ikjf/dot_general | solution.py:47
  111.7 9.9 %copy.54 = f32[8,4,8,1,1024]{4,2,3,1,0:T(8,128)S(1)} copy(f32[8,4,8,1,1024]{0,2,1,4,3:T(8,128)} %convolution_bitcast_fusion.1) | data formatting | bytes 2097152 | tf_op jit(solution)/shard_map/stack | solution.py:49
  121.6 0.0 copy-start
  121.6 0.1 pad_maximum_fusion
  121.7 2.0 %copy-done = f32[1024,1024]{1,0:T(8,128)S(1)} copy-done((f32[1024,1024]{1,0:T(8,128)S(1)}, f32[1024,1024]{1,0:T(8,128)}, u32[]{:S(2)}) %copy-start) | copy-done | bytes 4194328
  123.8 0.0 copy-start.1
  123.8 9.8 %fusion = f32[8,4,8,1024]{3,2,1,0:T(8,128)} fusion(f32[8,4,8,2048]{3,2,1,0:T(8,128)S(1)} %bitcast.32, f32[1024,1024]{1,0:T(8,128)} %get-tuple-element.10, f32[1024,1024]{1,0:T(8,128)S(1)} %copy-done), kind=kOutput, calls=%fused_computation.3 | convolution fusion | flops 6444548096 | bytes 11534336 | tf_op jit(solution)/shard_map/dot_general | solution.py:51
  133.6 0.0 reduce-scatter.2.cloned.1.call-update
  133.6 0.0 copy-done.1
  133.6 0.1 copy.56
  133.7 28.5 %reduce-scatter.2.cloned.1.call-done = f32[8,4,8,256]{3,2,1,0:T(8,128)} async-done(((f32[8,4,8,1024]{3,2,1,0:T(8,128)}), f32[8,4,8,256]{3,2,1,0:T(8,128)}) %reduce-scatter.2.cloned.1.call-update) | async-done | bytes 262160 | tf_op jit(solution)/shard_map/reduce_scatter | solution.py:53
  162.2 1.8 %broadcast_multiply_fusion = f32[8,4,8,256]{3,2,1,0:T(8,128)} fusion(f32[8,4,8,256]{3,2,1,0:T(8,128)} %reduce-scatter.2.cloned.1.call-done, f32[8,4]{1,0:T(8,128)S(1)} %copy.56), kind=kLoop, calls=%fused_computation.23 | loop fusion | flops 65536 | bytes 524416 | tf_op jit(solution)/shard_map/mul | solution.py:55
  (5 shorter events, 0.1 us)
Async XLA Ops:
  6.5 155.6 %reduce-scatter.2.cloned.1.call-start = ((), (), s32[]{:S(2)}) async-start(), calls=%async_computation.1 | async-start | bytes 1310720 | tf_op jit(solution)/shard_map/reduce_scatter | solution.py:53
  11.9 10.7 %collective-permute-start = (bf16[8,2,8,1024]{3,2,1,0:T(8,128)(2,1)S(1)}, bf16[8,2,8,1024]{3,2,1,0:T(8,128)(2,1)S(1)}, u32[]{:S(2)}, u32[]{:S(2)}) collective-permute-start(bf16[8,2,8,1024]{3,2,1,0:T(8,128)(2,1)S(1)} %get-tuple-element.6), channel_id=1, source_target_pairs={{4,0},{8,4},{12,8},{5,1},{9,5},{13,9},{6,2},{10,6},{14,10},{7,3},{... | collective-permute-start | bytes 786440 | tf_op jit(solution)/shard_map/ppermute | solution.py:19
  22.5 10.7 %collective-permute-start.1 = (bf16[8,2,8,1024]{3,2,1,0:T(8,128)(2,1)S(1)}, bf16[8,2,8,1024]{3,2,1,0:T(8,128)(2,1)S(1)}, u32[]{:S(2)}, u32[]{:S(2)}) collective-permute-start(bf16[8,2,8,1024]{3,2,1,0:T(8,128)(2,1)S(1)} %collective-permute-done), channel_id=1, source_target_pairs={{4,0},{8,4},{12,8},{5,1},{9,5},{13,9},{6,2},{10,6},{14,10},{7,3},{... | collective-permute-start | bytes 786440 | tf_op jit(solution)/shard_map/ppermute | solution.py:19
  33.3 20.8 %collective-permute-start.2 = (bf16[8,2,8,1024]{3,2,1,0:T(8,128)(2,1)S(1)}, bf16[8,2,8,1024]{3,2,1,0:T(8,128)(2,1)S(1)}, u32[]{:S(2)}, u32[]{:S(2)}) collective-permute-start(bf16[8,2,8,1024]{3,2,1,0:T(8,128)(2,1)S(1)} %collective-permute-done.1), channel_id=1, source_target_pairs={{4,0},{8,4},{12,8},{5,1},{9,5},{13,9},{6,2},{10,6},{14,10},{7,3},{... | collective-permute-start | bytes 786440 | tf_op jit(solution)/shard_map/ppermute | solution.py:19
  121.6 2.2 %copy-start = (f32[1024,1024]{1,0:T(8,128)S(1)}, f32[1024,1024]{1,0:T(8,128)}, u32[]{:S(2)}) copy-start(f32[1024,1024]{1,0:T(8,128)} %get-tuple-element.9) | copy-start | bytes 12582916
  123.8 9.8 %copy-start.1 = (s32[8,4]{0,1:T(4,128)S(1)}, s32[8,4]{0,1:T(4,128)}, u32[]{:S(2)}) copy-start(s32[8,4]{0,1:T(4,128)} %param.5) | copy-start | bytes 388
Sparse Core Ops, SparseCore 0:
  133.7 28.3 reduce-scatter.1
where the time goes:
time: 172 us; the launch traced here: 171 us
  local copies, waits for them, and re-layouts  53.9 us (31%)
  waiting for transfers between devices  37.9 us (22%)
  matrix products  34.7 us (20%)
  other arithmetic  24.4 us (14%)
  between operations  13.5 us (8%)
  starting transfers between devices  3.86 us (2%)
  blocking collectives  2.47 us (1%)
    reduce_scatter x1, waiting for transfers between devices, local(): lax.psum_scatter(partial_value, ('win', 'freq'), scatter_dimension=3, til...  28.5 us
    another operation x1, local copies, waits for them, and re-layouts, local(): stacked = jnp.stack(partners, axis=2)  22.7 us
    another operation x2, local copies, waits for them, and re-layouts, local(): cross = jnp.stack([real_part, imag_part], axis=3)  19.8 us
    cos x1, other arithmetic, lag_table(): return jnp.concatenate([jnp.cos(angle), -jnp.sin(angle)], axis=0)  19.5 us
    dot_general x1, matrix products, local(): jnp.einsum('wcif,wckjf->ikjf', swapped, stacked, preferred_element_type=j...  12.5 us
    dot_general x1, matrix products, local(): jnp.einsum('wcif,wckjf->ikjf', own, stacked, preferred_element_type=jnp.f...  12.4 us
    dot_general x1, matrix products, local(): jnp.dot(cross.reshape(-1, 2 * f_dev), table, precision=lax.Precision.HIGH...  9.81 us
    ppermute x3, waiting for transfers between devices, from_behind(): return lax.ppermute(block, axis, route)  9.38 us
  transfers between devices with their start and end apart: 4, of which 2 were waited for; matrix products, arithmetic and copies ran while one was open for 17% of the time, Pallas kernels for 0%

commit v1 on v0

v1 whole, which is shorter than its diff:
```python
import functools
import math

import jax
import jax.numpy as jnp
import numpy as np
from jax import lax
from jax.experimental import pallas as pl
from jax.experimental.pallas import tpu as pltpu
from jax.sharding import PartitionSpec as P

LAGS = 1024
F_LO = 60
NSAMP = 15000
EPS = 1e-06
LANES = 128
FINE = 16
MESH = pl.DeviceIdType.MESH


def turn_table(bins):
    offsets = np.arange(LAGS, dtype=np.int64) - LAGS // 2
    turns = np.remainder(np.asarray(bins, np.int64)[:, None] * offsets[None, :], NSAMP)
    angle = turns.astype(np.float64) * (2.0 * math.pi / NSAMP)
    return np.stack([np.cos(angle), np.sin(angle)]).astype(np.float32)


def split(x):
    high = x.astype(jnp.bfloat16)
    low = (x - high.astype(jnp.float32)).astype(jnp.bfloat16)
    return high, low


def kernel(reach, sizes, keep_ref, spec_ref, coarse_ref, fine_ref, out_ref,
           comm, own, power, power_in, coarse, table, lhs, partial, arrived,
           load_sem, power_send, power_recv, block_send, block_recv, sum_send, sum_recv):
    n_chan, n_win, n_freq = sizes
    w_dev, _, ch_dev, f_dev = spec_ref.shape
    chan, win, freq = (lax.axis_index(name) for name in ("chan", "win", "freq"))
    n_group = n_win * n_freq
    me = win * n_freq + freq
    lag_dev = LAGS // n_group
    rows = ch_dev * ch_dev

    def peer(step):
        g = lax.rem(me + step, n_group)
        return g, {"win": g // n_freq, "freq": lax.rem(g, n_freq)}

    barrier = pltpu.get_barrier_semaphore()
    for step in range(1, n_group):
        pl.semaphore_signal(barrier, inc=1, device_id=peer(step)[1], device_id_type=MESH)

    @pl.when(chan > 0)
    def _():
        pl.semaphore_signal(barrier, inc=1, device_id={"chan": chan - 1}, device_id_type=MESH)

    @pl.when(chan < n_chan - 1)
    def _():
        pl.semaphore_signal(barrier, inc=1, device_id={"chan": chan + 1}, device_id_type=MESH)

    groups = f_dev // FINE
    load = pltpu.make_async_copy(
        coarse_ref.at[:, pl.ds(pl.multiple_of(freq * groups, groups), groups)], coarse, load_sem)
    load.start()

    for w in range(w_dev):
        x = spec_ref[w].astype(jnp.float32)
        s = x[0] * x[0] + x[1] * x[1]
        total = s[:, :LANES]
        for q in range(1, f_dev // LANES):
            total = total + s[:, q * LANES:(q + 1) * LANES]
        power[w] = total

    inside = jnp.where(chan > 0, 1, 0) + jnp.where(chan < n_chan - 1, 1, 0)
    pl.semaphore_wait(barrier, n_group - 1 + inside)

    power_copies = []
    for step in range(1, n_freq):
        copy = pltpu.make_async_remote_copy(
            src_ref=power, dst_ref=power_in.at[step - 1],
            send_sem=power_send.at[step - 1], recv_sem=power_recv.at[step - 1],
            device_id={"freq": lax.rem(freq + step, n_freq)}, device_id_type=MESH)
        copy.start()
        power_copies.append(copy)
    for copy in power_copies:
        copy.wait()

    for w in range(w_dev):
        total = power[w]
        for step in range(1, n_freq):
            total = total + power_in[step - 1, w]
        mean = jnp.sum(total, axis=-1, keepdims=True) / (f_dev * n_freq)
        white = (spec_ref[w].astype(jnp.float32) * lax.rsqrt(mean + EPS)[None]).astype(jnp.bfloat16)
        comm[0, w] = white
        own[w] = white.astype(jnp.float32) * keep_ref[w].astype(jnp.float32)

    def block_copy(k):
        return pltpu.make_async_remote_copy(
            src_ref=comm.at[k], dst_ref=comm.at[k + 1],
            send_sem=block_send.at[k], recv_sem=block_recv.at[k],
            device_id={"chan": chan - 1}, device_id_type=MESH)

    @pl.when(chan > 0)
    def _():
        block_copy(0).start()

    load.wait()

    def make_table(a, carry):
        fine_cos, fine_sin = fine_ref[0], fine_ref[1]
        coarse_cos, coarse_sin = coarse[0, pl.ds(a, 1)], coarse[1, pl.ds(a, 1)]
        cos = coarse_cos * fine_cos - coarse_sin * fine_sin
        minus_sin = -(coarse_sin * fine_cos) - coarse_cos * fine_sin
        per = LANES // FINE
        row = pl.multiple_of((a // per) * (2 * LANES) + lax.rem(a, per) * FINE, FINE)
        for value, at in ((cos, row), (minus_sin, row + LANES)):
            high, low = split(value)
            at = pl.ds(pl.multiple_of(at, FINE), FINE)
            table[0, at] = high
            table[1, at] = low
        return carry

    lax.fori_loop(0, groups, make_table, 0)

    def sum_copy(k, step):
        g, where = peer(step)
        return pltpu.make_async_remote_copy(
            src_ref=partial.at[k, g], dst_ref=arrived.at[k, step - 1],
            send_sem=sum_send.at[k, step - 1], recv_sem=sum_recv.at[k, step - 1],
            device_id=where, device_id_type=MESH)

    def one_offset(k, carry):
        @pl.when(jnp.logical_and(k > 0, chan + k < n_chan))
        def _():
            block_copy(k - 1).wait_recv()

        @pl.when(jnp.logical_and(jnp.logical_and(k > 0, k < reach), jnp.logical_and(chan > 0, chan + k < n_chan)))
        def _():
            block_copy(k).start()

        @pl.when(chan + k < n_chan)
        def _():
            def cross(q, c):
                lanes = pl.ds(pl.multiple_of(q * LANES, LANES), LANES)
                partner = comm[k, :, :, :, lanes].astype(jnp.float32)
                for i in range(0, ch_dev, 2):
                    real, imag = [], []
                    for ii in (i, i + 1):
                        re = im = None
                        for w in range(w_dev):
                            a = jnp.broadcast_to(own[w, 0, pl.ds(ii, 1), lanes], (ch_dev, LANES))
                            b = jnp.broadcast_to(own[w, 1, pl.ds(ii, 1), lanes], (ch_dev, LANES))
                            p, r = partner[w, 0], partner[w, 1]
                            one, two = a * p + b * r, b * p - a * r
                            re = one if re is None else re + one
                            im = two if im is None else im + two
                        real.append(re)
                        imag.append(im)
                    for part, value in enumerate((real, imag)):
                        high, low = split(jnp.concatenate(value, axis=0))
                        at = pl.ds(pl.multiple_of(q * 2 * LANES + part * LANES, LANES), LANES)
                        lhs[pl.ds(i * ch_dev, 2 * ch_dev), at] = high
                        lhs[pl.ds(rows + i * ch_dev, 2 * ch_dev), at] = low
                return c

            lax.fori_loop(0, f_dev // LANES, cross, 0)
            for step in list(range(1, n_group)) + [0]:
                g, _ = peer(step)
                lags = pl.ds(pl.multiple_of(g * lag_dev, lag_dev), lag_dev)
                both = jnp.dot(lhs[...], table[0, :, lags], preferred_element_type=jnp.float32)
                rest = jnp.dot(lhs[pl.ds(0, rows)], table[1, :, lags], preferred_element_type=jnp.float32)
                partial[k, g] = both[:rows] + (both[rows:] + rest)
                if step:
                    sum_copy(k, step).start()

        return carry

    lax.fori_loop(0, reach + 1, one_offset, 0)

    for k in range(reach + 1):
        @pl.when(chan + k < n_chan)
        def _():
            total = partial[k, me]
            for step in range(1, n_group):
                sum_copy(k, step).wait_recv()
                total = total + arrived[k, step - 1]
            out_ref[:, k] = total.reshape(ch_dev, ch_dev, lag_dev)

        @pl.when(chan + k >= n_chan)
        def _():
            out_ref[:, k] = jnp.zeros((ch_dev, ch_dev, lag_dev), jnp.float32)

    for k in range(reach + 1):
        @pl.when(chan + k < n_chan)
        def _():
            for step in range(1, n_group):
                sum_copy(k, step).wait_send()

        if k < reach:
            @pl.when(jnp.logical_and(chan > 0, chan + k < n_chan))
            def _():
                block_copy(k).wait_send()


def local(spectra, keep, pair_mask):
    w_dev, _, ch_dev, f_dev = spectra.shape
    reach = pair_mask.shape[1] - 1
    n_chan, n_freq, n_win = (lax.axis_size(name) for name in ("chan", "freq", "win"))
    n_group = n_freq * n_win
    lag_dev = LAGS // n_group
    rows = ch_dev * ch_dev
    coarse = jnp.asarray(turn_table(F_LO + np.arange(0, f_dev * n_freq, FINE)))
    fine = jnp.asarray(turn_table(np.arange(FINE)))
    groups = f_dev // FINE
    vmem = pl.BlockSpec(memory_space=pltpu.VMEM)
    dma = pltpu.SemaphoreType.DMA
    lagsum = pl.pallas_call(
        functools.partial(kernel, reach, (n_chan, n_win, n_freq)),
        out_shape=jax.ShapeDtypeStruct((ch_dev, reach + 1, ch_dev, lag_dev), jnp.float32),
        in_specs=[pl.BlockSpec(memory_space=pltpu.SMEM), vmem, pl.BlockSpec(memory_space=pl.ANY), vmem],
        out_specs=vmem,
        scratch_shapes=[
            pltpu.VMEM((reach + 1,) + spectra.shape, jnp.bfloat16),
            pltpu.VMEM(spectra.shape, jnp.float32),
            pltpu.VMEM((w_dev, ch_dev, LANES), jnp.float32),
            pltpu.VMEM((n_freq - 1, w_dev, ch_dev, LANES), jnp.float32),
            pltpu.VMEM((2, groups, LAGS), jnp.float32),
            pltpu.VMEM((2, 2 * f_dev, LAGS), jnp.bfloat16),
            pltpu.VMEM((2 * rows, 2 * f_dev), jnp.bfloat16),
            pltpu.VMEM((reach + 1, n_group, rows, lag_dev), jnp.float32),
            pltpu.VMEM((reach + 1, n_group - 1, rows, lag_dev), jnp.float32),
            dma,
            dma((n_freq - 1,)),
            dma((n_freq - 1,)),
            dma((reach,)),
            dma((reach,)),
            dma((reach + 1, n_group - 1)),
            dma((reach + 1, n_group - 1)),
        ],
        compiler_params=pltpu.CompilerParams(
            collective_id=0, has_side_effects=True, vmem_limit_bytes=60 * 1024 * 1024),
    )(keep, spectra, coarse, fine)
    scale = 1.0 / math.sqrt(w_dev * n_win * f_dev * n_freq)
    return lagsum * scale * pair_mask.astype(jnp.float32)[:, :, None, None]


def solution(mesh):
    in_specs = (
        P("win", None, ("fibre", "chan"), "freq"),
        P(("fibre", "win")),
        P(("fibre", "chan"), None),
    )
    out_specs = P(("fibre", "chan"), None, None, ("win", "freq"))
    return jax.shard_map(local, mesh=mesh, in_specs=in_specs, out_specs=out_specs, check_vma=False)
```

time: 172 us -> 37.1 us (0.22)
  local copies, waits for them, and re-layouts: 53.9 us -> 0.08 us
  waiting for transfers between devices: 37.9 us -> 0 us
  matrix products: 34.7 us -> 0 us
  Pallas kernels: 0 us -> 34.4 us
  other arithmetic: 24.4 us -> 2.44 us
  between operations: 13.5 us -> 0.01 us
  starting transfers between devices: 3.86 us -> 0 us
  blocking collectives: 2.47 us -> 0 us
    another operation x3 -> x0, local copies, waits for them, and re-layouts: 42.4 us -> none  [the longest x1 22.7 us: local(): stacked = jnp.stack(partners, axis=2)]
    dot_general x3 -> x0, matrix products: 34.7 us -> none  [the longest x1 12.5 us: local(): jnp.einsum('wcif,wckjf->ikjf', swapped, stacked, preferred_element_type=j...]
    pallas_call x0 -> x1, Pallas kernels: none -> 34.4 us  [local(): pl.pallas_call(functools.partial(kernel, reach, (n_chan, n_win, n_freq)),...]
    reduce_scatter x1 -> x0, waiting for transfers between devices: 28.5 us -> none  [local(): lax.psum_scatter(partial_value, ('win', 'freq'), scatter_dimension=3, til...]
    cos x1 -> x0, other arithmetic: 19.5 us -> none  [lag_table(): return jnp.concatenate([jnp.cos(angle), -jnp.sin(angle)], axis=0)]
    ppermute x3 -> x0, waiting for transfers between devices: 9.38 us -> none  [from_behind(): return lax.ppermute(block, axis, route)]
    mul x1 -> x0, local copies, waits for them, and re-layouts: 4.68 us -> none  [local(): own = white * keep.astype(jnp.bfloat16)[:, None, None, None]]
    concatenate x1 -> x0, local copies, waits for them, and re-layouts: 4.67 us -> none  [local(): swapped = jnp.concatenate([own[:, 1:2], -own[:, 0:1]], axis=1)]
  transfers between devices with their start and end apart: 4 -> 0, of which waited for: 2 -> 0; matrix products, arithmetic and copies ran while one was open for 17% -> 0% of each run, Pallas kernels for 0% -> 0%
where the time goes in v1:
time: 37.1 us; the launch traced here: 36.9 us
  Pallas kernels  34.4 us (93%)
  other arithmetic  2.44 us (7%)
    pallas_call x1, Pallas kernels, local(): pl.pallas_call(functools.partial(kernel, reach, (n_chan, n_win, n_freq)),...  34.4 us
    mul x2, other arithmetic, local(): return lagsum * scale * pair_mask.astype(jnp.float32)[:, :, None, None]  2.44 us

profile of v1, /device:TPU:1, one launch (start us, length us, event | category | flops | bytes accessed | tf_op | source)
XLA Modules:
  0.0 36.9 jit_solution(11547604208847241121)
XLA Ops:
  0.0 0.7 %convert_multiply_fusion = f32[8,4]{0,1:T(4,128)S(1)} fusion(s32[8,4]{0,1:T(4,128)} %param.7), kind=kLoop, calls=%fused_computation.1 | loop fusion | flops 64 | bytes 256 | tf_op jit(solution)/shard_map/mul | solution.py:244
  0.7 0.1 copy.6
  0.8 34.4 %shard_map.55 = f32[8,4,8,256]{3,2,1,0:T(8,128)} custom-call(s32[8]{0:T(128)} %keep_ref.1, bf16[8,2,8,1024]{3,2,1,0:T(8,128)(2,1)} %spec_ref.1, f32[2,128,1024]{2,1,0:T(8,128)} %constant.6.clone.coarse_ref, f32[2,16,1024]{2,1,0:T(8,128)} %constant.7.clone.fine_ref), custom_call_target="tpu_custom_call" | custom-call | tf_op jit(solution)/shard_map/pallas_call | solution.py:217
  35.2 1.8 %broadcast_multiply_fusion = f32[8,4,8,256]{3,2,1,0:T(8,128)} fusion(f32[8,4,8,256]{3,2,1,0:T(8,128)} %shard_map.55, f32[8,4]{1,0:T(8,128)S(1)} %copy.6), kind=kLoop, calls=%fused_computation | loop fusion | flops 65536 | bytes 524416 | tf_op jit(solution)/shard_map/mul | solution.py:244

commit v2 on v1

v2 whole, which is shorter than its diff:
```python
import functools
import math

import jax
import jax.numpy as jnp
import numpy as np
from jax import lax
from jax.experimental import pallas as pl
from jax.experimental.pallas import tpu as pltpu
from jax.sharding import PartitionSpec as P

LAGS = 1024
F_LO = 60
NSAMP = 15000
EPS = 1e-06
LANES = 128
FINE = 16
PIECES = 4
EARLY = 2
MESH = pl.DeviceIdType.MESH


def turn_table(bins):
    offsets = np.arange(LAGS, dtype=np.int64) - LAGS // 2
    turns = np.remainder(np.asarray(bins, np.int64)[:, None] * offsets[None, :], NSAMP)
    angle = turns.astype(np.float64) * (2.0 * math.pi / NSAMP)
    return np.stack([np.cos(angle), np.sin(angle)]).astype(np.float32)


def split(x):
    high = x.astype(jnp.bfloat16)
    low = (x - high.astype(jnp.float32)).astype(jnp.bfloat16)
    return high, low


def kernel(reach, sizes, keep_ref, mask_ref, spec_ref, coarse_ref, fine_ref, out_ref,
           comm, scales, gains, own, power, power_in, coarse, fine, table, lhs, partial, arrived, result,
           spec_sem, load_sem, out_sem, power_send, power_recv, scale_send, scale_recv, block_send, block_recv, sum_send, sum_recv):
    n_chan, n_win, n_freq = sizes
    w_dev, _, ch_dev, f_dev = spec_ref.shape
    chan, win, freq = (lax.axis_index(name) for name in ("chan", "win", "freq"))
    n_group = n_win * n_freq
    me = win * n_freq + freq
    lag_dev = LAGS // n_group
    rows = ch_dev * ch_dev
    f_piece = f_dev // PIECES
    scale = 1.0 / math.sqrt(w_dev * n_win * f_dev * n_freq)

    def peer(step):
        g = lax.rem(me + step, n_group)
        return g, {"win": g // n_freq, "freq": lax.rem(g, n_freq)}

    barrier = pltpu.get_barrier_semaphore()

    @pl.when(chan > 0)
    def _():
        pl.semaphore_signal(barrier, inc=1, device_id={"chan": chan - 1}, device_id_type=MESH)

    @pl.when(chan < n_chan - 1)
    def _():
        pl.semaphore_signal(barrier, inc=1, device_id={"chan": chan + 1}, device_id_type=MESH)

    for step in range(1, n_group):
        pl.semaphore_signal(barrier, inc=1, device_id=peer(step)[1], device_id_type=MESH)

    groups = f_dev // FINE
    loads = [pltpu.make_async_copy(
        spec_ref.at[:, :, :, pl.ds(c * f_piece, f_piece)], comm.at[0, c], spec_sem.at[c]) for c in range(PIECES)]
    tables = [
        pltpu.make_async_copy(
            coarse_ref.at[:, pl.ds(pl.multiple_of(freq * groups, groups), groups)], coarse, load_sem.at[0]),
        pltpu.make_async_copy(fine_ref, fine, load_sem.at[1])]
    for load in loads + tables:
        load.start()

    inside = jnp.where(chan > 0, 1, 0) + jnp.where(chan < n_chan - 1, 1, 0)
    pl.semaphore_wait(barrier, n_group - 1 + inside)

    def piece_copy(k, c, source=None):
        return pltpu.make_async_remote_copy(
            src_ref=comm.at[k, c] if source is None else source.at[:, :, :, pl.ds(c * f_piece, f_piece)],
            dst_ref=comm.at[k + 1, c],
            send_sem=block_send.at[k, c], recv_sem=block_recv.at[k, c],
            device_id={"chan": chan - 1}, device_id_type=MESH)

    def scale_copy(k):
        return pltpu.make_async_remote_copy(
            src_ref=scales.at[k], dst_ref=scales.at[k + 1],
            send_sem=scale_send.at[k], recv_sem=scale_recv.at[k],
            device_id={"chan": chan - 1}, device_id_type=MESH)

    @pl.when(chan > 0)
    def _():
        for c in range(EARLY):
            piece_copy(0, c, spec_ref).start()

    for load in loads:
        load.wait()

    for w in range(w_dev):
        total = None
        for c in range(PIECES):
            x = comm[0, c, w].astype(jnp.float32)
            s = x[0] * x[0] + x[1] * x[1]
            for q in range(f_piece // LANES):
                term = s[:, q * LANES:(q + 1) * LANES]
                total = term if total is None else total + term
        power[w] = total

    power_copies = []
    for step in range(1, n_freq):
        copy = pltpu.make_async_remote_copy(
            src_ref=power, dst_ref=power_in.at[step - 1],
            send_sem=power_send.at[step - 1], recv_sem=power_recv.at[step - 1],
            device_id={"freq": lax.rem(freq + step, n_freq)}, device_id_type=MESH)
        copy.start()
        power_copies.append(copy)

    for copy in power_copies:
        copy.wait()

    lane = lax.broadcasted_iota(jnp.int32, (ch_dev, LANES), 1)
    tile = jnp.zeros((ch_dev, LANES), jnp.float32)
    for w in range(w_dev):
        total = power[w]
        for step in range(1, n_freq):
            total = total + power_in[step - 1, w]
        mean = jnp.sum(total, axis=-1, keepdims=True) / (f_dev * n_freq)
        tile = jnp.where(lane == w, lax.rsqrt(mean + EPS), tile)
    scales[0] = tile

    @pl.when(chan > 0)
    def _():
        scale_copy(0).start()
        for c in range(EARLY, PIECES):
            piece_copy(0, c, spec_ref).start()

    def spread(k):
        tile = scales[k]
        for w in range(w_dev):
            gains[w] = jnp.broadcast_to(tile[:, w:w + 1], (ch_dev, LANES))

    spread(0)
    for w in range(w_dev):
        gain = jnp.concatenate([gains[w]] * (f_piece // LANES), axis=1)
        kept = keep_ref[w].astype(jnp.float32)
        for c in range(PIECES):
            white = (comm[0, c, w].astype(jnp.float32) * gain[None]).astype(jnp.bfloat16)
            own[w, :, :, pl.ds(c * f_piece, f_piece)] = white.astype(jnp.float32) * kept

    for load in tables:
        load.wait()

    def make_table(a, carry):
        fine_cos, fine_sin = fine[0], fine[1]
        coarse_cos, coarse_sin = coarse[0, pl.ds(a, 1)], coarse[1, pl.ds(a, 1)]
        cos = coarse_cos * fine_cos - coarse_sin * fine_sin
        minus_sin = -(coarse_sin * fine_cos) - coarse_cos * fine_sin
        per = LANES // FINE
        row = pl.multiple_of((a // per) * (2 * LANES) + lax.rem(a, per) * FINE, FINE)
        for value, at in ((cos, row), (minus_sin, row + LANES)):
            high, low = split(value)
            at = pl.ds(pl.multiple_of(at, FINE), FINE)
            table[0, at] = high
            table[1, at] = low
        return carry

    lax.fori_loop(0, groups, make_table, 0)

    def sum_copy(k, step):
        g, where = peer(step)
        return pltpu.make_async_remote_copy(
            src_ref=partial.at[k, g], dst_ref=arrived.at[k, step - 1],
            send_sem=sum_send.at[k, step - 1], recv_sem=sum_recv.at[k, step - 1],
            device_id=where, device_id_type=MESH)

    def receive(k, pieces, with_scale):
        @pl.when(chan + k < n_chan)
        def _():
            onward = jnp.logical_and(k < reach, chan > 0)
            for c in pieces:
                piece_copy(k - 1, c).wait_recv()

                @pl.when(onward)
                def _():
                    piece_copy(k, c).start()

            if with_scale:
                scale_copy(k - 1).wait_recv()

                @pl.when(onward)
                def _():
                    scale_copy(k).start()

    def compute(k, first, last):
        start = first * f_piece
        depth = (last - first) * f_piece

        def cross(q, c):
            lanes = pl.ds(pl.multiple_of(start + q * LANES, LANES), LANES)
            per = f_piece // LANES
            piece = first + q // per
            within = pl.ds(pl.multiple_of(lax.rem(q, per) * LANES, LANES), LANES)
            partner = []
            for w in range(w_dev):
                white = comm[k, piece, w, :, :, within].astype(jnp.float32) * gains[w][None]
                partner.append(white.astype(jnp.bfloat16).astype(jnp.float32))
            for i in range(0, ch_dev, 2):
                real, imag = [], []
                for ii in (i, i + 1):
                    re = im = None
                    for w in range(w_dev):
                        a = jnp.broadcast_to(own[w, 0, pl.ds(ii, 1), lanes], (ch_dev, LANES))
                        b = jnp.broadcast_to(own[w, 1, pl.ds(ii, 1), lanes], (ch_dev, LANES))
                        p, r = partner[w][0], partner[w][1]
                        one, two = a * p + b * r, b * p - a * r
                        re = one if re is None else re + one
                        im = two if im is None else im + two
                    real.append(re)
                    imag.append(im)
                for part, value in enumerate((real, imag)):
                    high, low = split(jnp.concatenate(value, axis=0))
                    at = pl.ds(pl.multiple_of(2 * start + q * 2 * LANES + part * LANES, LANES), LANES)
                    lhs[pl.ds(i * ch_dev, 2 * ch_dev), at] = high
                    lhs[pl.ds(rows + i * ch_dev, 2 * ch_dev), at] = low
            return c

        lax.fori_loop(0, depth // LANES, cross, 0)
        deep = pl.ds(2 * start, 2 * depth)
        for step in list(range(1, n_group)) + [0]:
            g, _ = peer(step)
            lags = pl.ds(pl.multiple_of(g * lag_dev, lag_dev), lag_dev)
            both = jnp.dot(lhs[:, deep], table[0, deep, lags], preferred_element_type=jnp.float32)
            rest = jnp.dot(lhs[pl.ds(0, rows), deep], table[1, deep, lags], preferred_element_type=jnp.float32)
            value = both[:rows] + (both[rows:] + rest)
            partial[k, g] = value if first == 0 else partial[k, g] + value
            if step and last == PIECES:
                sum_copy(k, step).start()

    def out_copy(k):
        return pltpu.make_async_copy(result.at[k], out_ref.at[:, k], out_sem.at[k])

    def finish(k):
        @pl.when(chan + k < n_chan)
        def _():
            total = partial[k, me]
            for step in range(1, n_group):
                sum_copy(k, step).wait_recv()
                total = total + arrived[k, step - 1]
            for c in range(ch_dev):
                result[k, c] = total[c * ch_dev:(c + 1) * ch_dev] * (mask_ref[k, c].astype(jnp.float32) * scale)

        @pl.when(chan + k >= n_chan)
        def _():
            result[k] = jnp.zeros((ch_dev, ch_dev, lag_dev), jnp.float32)

        out_copy(k).start()

    receive(1, range(EARLY), True)

    def one_offset(k, carry):
        @pl.when(chan + k < n_chan)
        def _():
            spread(k)
            compute(k, 0, EARLY)

        for c in range(EARLY, PIECES):
            @pl.when(k > 0)
            def _():
                receive(k, (c,), False)

            @pl.when(chan + k < n_chan)
            def _():
                compute(k, c, c + 1)

        @pl.when(k > 0)
        def _():
            @pl.when(k < reach)
            def _():
                receive(k + 1, range(EARLY), True)

            finish(k - 1)

        return carry

    lax.fori_loop(0, reach + 1, one_offset, 0)
    finish(reach)

    for k in range(reach + 1):
        out_copy(k).wait()

        @pl.when(chan + k < n_chan)
        def _():
            for step in range(1, n_group):
                sum_copy(k, step).wait_send()

        if k < reach:
            @pl.when(jnp.logical_and(chan > 0, chan + k < n_chan))
            def _():
                scale_copy(k).wait_send()
                for c in range(PIECES):
                    piece_copy(k, c, spec_ref if k == 0 else None).wait_send()


def local(spectra, keep, pair_mask):
    w_dev, _, ch_dev, f_dev = spectra.shape
    reach = pair_mask.shape[1] - 1
    n_chan, n_freq, n_win = (lax.axis_size(name) for name in ("chan", "freq", "win"))
    n_group = n_freq * n_win
    lag_dev = LAGS // n_group
    rows = ch_dev * ch_dev
    coarse = jnp.asarray(turn_table(F_LO + np.arange(0, f_dev * n_freq, FINE)))
    fine = jnp.asarray(turn_table(np.arange(FINE)))
    groups = f_dev // FINE
    smem = pl.BlockSpec(memory_space=pltpu.SMEM)
    hbm = pl.BlockSpec(memory_space=pl.ANY)
    dma = pltpu.SemaphoreType.DMA
    return pl.pallas_call(
        functools.partial(kernel, reach, (n_chan, n_win, n_freq)),
        out_shape=jax.ShapeDtypeStruct((ch_dev, reach + 1, ch_dev, lag_dev), jnp.float32),
        in_specs=[smem, smem, hbm, hbm, hbm],
        out_specs=hbm,
        scratch_shapes=[
            pltpu.VMEM((reach + 1, PIECES, w_dev, 2, ch_dev, f_dev // PIECES), jnp.bfloat16),
            pltpu.VMEM((reach + 1, ch_dev, LANES), jnp.float32),
            pltpu.VMEM((w_dev, ch_dev, LANES), jnp.float32),
            pltpu.VMEM(spectra.shape, jnp.float32),
            pltpu.VMEM((w_dev, ch_dev, LANES), jnp.float32),
            pltpu.VMEM((n_freq - 1, w_dev, ch_dev, LANES), jnp.float32),
            pltpu.VMEM((2, groups, LAGS), jnp.float32),
            pltpu.VMEM((2, FINE, LAGS), jnp.float32),
            pltpu.VMEM((2, 2 * f_dev, LAGS), jnp.bfloat16),
            pltpu.VMEM((2 * rows, 2 * f_dev), jnp.bfloat16),
            pltpu.VMEM((reach + 1, n_group, rows, lag_dev), jnp.float32),
            pltpu.VMEM((reach + 1, n_group - 1, rows, lag_dev), jnp.float32),
            pltpu.VMEM((reach + 1, ch_dev, ch_dev, lag_dev), jnp.float32),
            dma((PIECES,)),
            dma((2,)),
            dma((reach + 1,)),
            dma((n_freq - 1,)),
            dma((n_freq - 1,)),
            dma((reach,)),
            dma((reach,)),
            dma((reach, PIECES)),
            dma((reach, PIECES)),
            dma((reach + 1, n_group - 1)),
            dma((reach + 1, n_group - 1)),
        ],
        compiler_params=pltpu.CompilerParams(
            collective_id=0, has_side_effects=True, vmem_limit_bytes=60 * 1024 * 1024),
    )(keep, pair_mask.T, spectra, coarse, fine)


def solution(mesh):
    in_specs = (
        P("win", None, ("fibre", "chan"), "freq"),
        P(("fibre", "win")),
        P(("fibre", "chan"), None),
    )
    out_specs = P(("fibre", "chan"), None, None, ("win", "freq"))
    return jax.shard_map(local, mesh=mesh, in_specs=in_specs, out_specs=out_specs, check_vma=False)
```

time: 37.1 us -> 32 us (0.86)
  Pallas kernels: 34.4 us -> 30.1 us
  other arithmetic: 2.44 us -> 0 us
  local copies, waits for them, and re-layouts: 0.08 us -> 1.67 us
    pallas_call x1, Pallas kernels: 34.4 us -> 30.1 us  [local(): pl.pallas_call(functools.partial(kernel, reach, (n_chan, n_win, n_freq)),...]
    mul x2 -> x0, other arithmetic: 2.44 us -> none  [local(): return lagsum * scale * pair_mask.astype(jnp.float32)[:, :, None, None]]
    unnamed x0 -> x1, local copies, waits for them, and re-layouts: none -> 1.67 us
where the time goes in v2:
time: 32 us; the launch traced here: 31.8 us
  Pallas kernels  30.1 us (94%)
  local copies, waits for them, and re-layouts  1.67 us (5%)
    pallas_call x1, Pallas kernels, local(): pl.pallas_call(functools.partial(kernel, reach, (n_chan, n_win, n_freq)),...  30.1 us
    unnamed x1, local copies, waits for them, and re-layouts  1.67 us

profile of v2, /device:TPU:1, one launch (start us, length us, event | category | flops | bytes accessed | tf_op | source)
XLA Modules:
  0.0 31.8 jit_solution(8068468367297543481)
XLA Ops:
  0.0 30.1 %shard_map.55 = f32[8,4,8,256]{3,2,1,0:T(8,128)} custom-call(s32[8]{0:T(128)} %keep_ref.1, s32[4,8]{1,0:T(4,128)} %bitcast.1, bf16[8,2,8,1024]{3,2,1,0:T(8,128)(2,1)} %spec_ref.1, f32[2,128,1024]{2,1,0:T(8,128)} %constant.4.clone.coarse_ref, f32[2,16,1024]{2,1,0:T(8,128)} %constant.5.clone.fine_ref), custom_call_target="tpu_custom_call" | custom-call | tf_op jit(solution)/shard_map/pallas_call | solution.py:318
  30.1 1.7 %copy.7 = f32[8,4,8,256]{3,2,1,0:T(8,128)} copy(f32[8,4,8,256]{3,2,1,0:T(8,128)} %shard_map.55) | data formatting | bytes 524288

commit v3 on v2

--- a/solution.py
+++ b/solution.py
@@ -34,8 +34,8 @@
 
 
 def kernel(reach, sizes, keep_ref, mask_ref, spec_ref, coarse_ref, fine_ref, out_ref,
-           comm, scales, gains, own, power, power_in, coarse, fine, table, lhs, partial, arrived, result,
-           spec_sem, load_sem, out_sem, power_send, power_recv, scale_send, scale_recv, block_send, block_recv, sum_send, sum_recv):
+           comm, scales, gains, own, power, power_in, coarse, fine, table, lhs, partial, arrived,
+           spec_sem, load_sem, power_send, power_recv, scale_send, scale_recv, block_send, block_recv, sum_send, sum_recv):
     n_chan, n_win, n_freq = sizes
     w_dev, _, ch_dev, f_dev = spec_ref.shape
     chan, win, freq = (lax.axis_index(name) for name in ("chan", "win", "freq"))
@@ -237,9 +237,6 @@
             if step and last == PIECES:
                 sum_copy(k, step).start()
 
-    def out_copy(k):
-        return pltpu.make_async_copy(result.at[k], out_ref.at[:, k], out_sem.at[k])
-
     def finish(k):
         @pl.when(chan + k < n_chan)
         def _():
@@ -248,13 +245,11 @@
                 sum_copy(k, step).wait_recv()
                 total = total + arrived[k, step - 1]
             for c in range(ch_dev):
-                result[k, c] = total[c * ch_dev:(c + 1) * ch_dev] * (mask_ref[k, c].astype(jnp.float32) * scale)
+                out_ref[c, k] = total[c * ch_dev:(c + 1) * ch_dev] * (mask_ref[k, c].astype(jnp.float32) * scale)
 
         @pl.when(chan + k >= n_chan)
         def _():
-            result[k] = jnp.zeros((ch_dev, ch_dev, lag_dev), jnp.float32)
-
-        out_copy(k).start()
+            out_ref[:, k] = jnp.zeros((ch_dev, ch_dev, lag_dev), jnp.float32)
 
     receive(1, range(EARLY), True)
 
@@ -287,8 +282,6 @@
     finish(reach)
 
     for k in range(reach + 1):
-        out_copy(k).wait()
-
         @pl.when(chan + k < n_chan)
         def _():
             for step in range(1, n_group):
@@ -317,9 +310,9 @@
     dma = pltpu.SemaphoreType.DMA
     return pl.pallas_call(
         functools.partial(kernel, reach, (n_chan, n_win, n_freq)),
-        out_shape=jax.ShapeDtypeStruct((ch_dev, reach + 1, ch_dev, lag_dev), jnp.float32),
+        out_shape=pltpu.VMEM((ch_dev, reach + 1, ch_dev, lag_dev), jnp.float32),
         in_specs=[smem, smem, hbm, hbm, hbm],
-        out_specs=hbm,
+        out_specs=pl.BlockSpec(memory_space=pltpu.VMEM),
         scratch_shapes=[
             pltpu.VMEM((reach + 1, PIECES, w_dev, 2, ch_dev, f_dev // PIECES), jnp.bfloat16),
             pltpu.VMEM((reach + 1, ch_dev, LANES), jnp.float32),
@@ -333,10 +326,8 @@
             pltpu.VMEM((2 * rows, 2 * f_dev), jnp.bfloat16),
             pltpu.VMEM((reach + 1, n_group, rows, lag_dev), jnp.float32),
             pltpu.VMEM((reach + 1, n_group - 1, rows, lag_dev), jnp.float32),
-            pltpu.VMEM((reach + 1, ch_dev, ch_dev, lag_dev), jnp.float32),
             dma((PIECES,)),
             dma((2,)),
-            dma((reach + 1,)),
             dma((n_freq - 1,)),
             dma((n_freq - 1,)),
             dma((reach,)),

time: 32 us -> 30.4 us (0.950)
  local copies, waits for them, and re-layouts: 1.67 us -> 0.71 us
  Pallas kernels: 30.1 us -> 29.5 us
    unnamed x1, local copies, waits for them, and re-layouts: 1.67 us -> 0.71 us
    pallas_call x1, Pallas kernels: 30.1 us -> 29.5 us  [local(): pl.pallas_call(functools.partial(kernel, reach, (n_chan, n_win, n_freq)),...]
where the time goes in v3:
time: 30.4 us; the launch traced here: 30.2 us
  Pallas kernels  29.5 us (97%)
  local copies, waits for them, and re-layouts  0.71 us (2%)
    pallas_call x1, Pallas kernels, local(): pl.pallas_call(functools.partial(kernel, reach, (n_chan, n_win, n_freq)),...  29.5 us
    unnamed x1, local copies, waits for them, and re-layouts  0.71 us

profile of v3, /device:TPU:1, one launch (start us, length us, event | category | flops | bytes accessed | tf_op | source)
XLA Modules:
  0.0 30.2 jit_solution(6104337538501405449)
XLA Ops:
  0.0 29.5 %shard_map.55 = f32[8,4,8,256]{3,2,1,0:T(8,128)S(1)} custom-call(s32[8]{0:T(128)} %keep_ref.1, s32[4,8]{1,0:T(4,128)} %bitcast.1, bf16[8,2,8,1024]{3,2,1,0:T(8,128)(2,1)} %spec_ref.1, f32[2,128,1024]{2,1,0:T(8,128)} %constant.4.clone.coarse_ref, f32[2,16,1024]{2,1,0:T(8,128)} %constant.5.clone.fine_ref), custom_call_target="tpu_custom_call" | custom-call | tf_op jit(solution)/shard_map/pallas_call | solution.py:311
  29.5 0.7 %copy.7 = f32[8,4,8,256]{3,2,1,0:T(8,128)} copy(f32[8,4,8,256]{3,2,1,0:T(8,128)S(1)} %shard_map.55) | data formatting | bytes 524288

commit v4 on v3

--- a/solution.py
+++ b/solution.py
@@ -15,8 +15,8 @@
 EPS = 1e-06
 LANES = 128
 FINE = 16
-PIECES = 4
-EARLY = 2
+PIECES = 2
+EARLY = 1
 MESH = pl.DeviceIdType.MESH
 
 
@@ -47,8 +47,9 @@
     scale = 1.0 / math.sqrt(w_dev * n_win * f_dev * n_freq)
 
     def peer(step):
-        g = lax.rem(me + step, n_group)
-        return g, {"win": g // n_freq, "freq": lax.rem(g, n_freq)}
+        to_win = lax.rem(win + step // n_freq, n_win)
+        to_freq = lax.rem(freq + step % n_freq, n_freq)
+        return to_win * n_freq + to_freq, {"win": to_win, "freq": to_freq}
 
     barrier = pltpu.get_barrier_semaphore()
 
@@ -227,7 +228,7 @@
 
         lax.fori_loop(0, depth // LANES, cross, 0)
         deep = pl.ds(2 * start, 2 * depth)
-        for step in list(range(1, n_group)) + [0]:
+        for step in [*range(n_freq, n_group), *range(1, n_freq), 0]:
             g, _ = peer(step)
             lags = pl.ds(pl.multiple_of(g * lag_dev, lag_dev), lag_dev)
             both = jnp.dot(lhs[:, deep], table[0, deep, lags], preferred_element_type=jnp.float32)

time: 30.4 us -> 30.1 us (level)
  no operation moved by 1% of the time
where the time goes in v4:
time: 30.1 us; the launch traced here: 29.9 us
  Pallas kernels  29.2 us (97%)
  local copies, waits for them, and re-layouts  0.71 us (2%)
    pallas_call x1, Pallas kernels, local(): pl.pallas_call(functools.partial(kernel, reach, (n_chan, n_win, n_freq)),...  29.2 us
    unnamed x1, local copies, waits for them, and re-layouts  0.71 us

profile of v4, /device:TPU:1, one launch (start us, length us, event | category | flops | bytes accessed | tf_op | source)
XLA Modules:
  0.0 29.9 jit_solution(7423088888269241867)
XLA Ops:
  0.0 29.2 %shard_map.55 = f32[8,4,8,256]{3,2,1,0:T(8,128)S(1)} custom-call(s32[8]{0:T(128)} %keep_ref.1, s32[4,8]{1,0:T(4,128)} %bitcast.1, bf16[8,2,8,1024]{3,2,1,0:T(8,128)(2,1)} %spec_ref.1, f32[2,128,1024]{2,1,0:T(8,128)} %constant.4.clone.coarse_ref, f32[2,16,1024]{2,1,0:T(8,128)} %constant.5.clone.fine_ref), custom_call_target="tpu_custom_call" | custom-call | tf_op jit(solution)/shard_map/pallas_call | solution.py:312
  29.2 0.7 %copy.7 = f32[8,4,8,256]{3,2,1,0:T(8,128)} copy(f32[8,4,8,256]{3,2,1,0:T(8,128)S(1)} %shard_map.55) | data formatting | bytes 524288
